TPU v7x, 512 devices: a whole 4x8x8 slice. The times are simulated.
512 devices in a mesh: seq: 64 (over x, z, core), rep: 8 (over y).
Axes of the slice: x: 4, y: 8, z: 8, core: 2. Of those that a mesh axis runs over, the one named last changes fastest.
Arguments:
- token_ids: int32 [32, 4], P('rep'), parts along dimension 0, may hold values from 0 to 24703
- cache_lengths: int32 [32], P('rep'), parts along dimension 0, may hold values from 1 to 8192, 8216 in all
- embed_table: bfloat16 [2048, 24704], P('seq'), may hold values from -0.119628906 to 0.119628906
- key_cache: bfloat16 [32, 8192, 512], P('rep', 'seq'), parts along dimension 0, may hold values from -4000 to 4000
- value_cache: bfloat16 [32, 8192, 512], P('rep', 'seq'), parts along dimension 0, may hold values from -24 to 24
- norm_attn: bfloat16 [2048], replicated, may hold values from 0.25 to 1.75
- norm_mlp: bfloat16 [2048], replicated, may hold values from 0.25 to 1.75
- w_qkv: bfloat16 [2048, 3072], P(None, 'seq'), may hold values from -0.125 to 0.125
- w_out: bfloat16 [2048, 2048], P(None, 'seq'), may hold values from -0.125 to 0.125
- w_gate: bfloat16 [2048, 8192], P(None, 'seq'), may hold values from -0.125 to 0.125
- w_up: bfloat16 [2048, 8192], P(None, 'seq'), may hold values from -0.125 to 0.125
- w_down: bfloat16 [8192, 2048], P('seq'), may hold values from -0.0625 to 0.0625
Outputs:
- layer_out: bfloat16 [32, 4, 2048], P('rep'), parts along dimension 0
There are 8 independent parts, one for each index of `rep`. A program takes and returns all parts, laid end to end along the dimension named above; an argument that names none is the same for every part. Nothing has to cross between parts.
All inputs are finite; a program needn't handle non-finite values.
Results may differ from a plain program's by a relative error of at most 0.012.
The roundings to bfloat16 on the way count: a program that leaves them out, or rounds other values in their place, can miss the bound.
Values may be sent and summed in bfloat16 or wider, within the bound.
A program may use at most 128 MiB of HBM per device.

v0:
```python
import jax
import jax.numpy as jnp
from jax import lax
from jax.sharding import PartitionSpec as P

H = 32
KVH = 8
HD = 64
STEPS = 4
norm_epsilon = 1e-05
embed_factor = 12.0
score_factor = 0.015625
branch_factor = 0.22
rope_base = 10000000.0
masked_floor = -1e30


def rms_scale(resid, gain):
    mean_square = jnp.mean(resid * resid, axis=-1, keepdims=True)
    return resid * lax.rsqrt(mean_square + norm_epsilon) * gain.astype(jnp.float32)


def rotate(vectors, where):
    half = vectors.shape[-1] // 2
    freqs = rope_base ** (-2.0 * jnp.arange(half, dtype=jnp.float32) / vectors.shape[-1])
    angle = where[..., None] * freqs
    cosine = jnp.cos(angle)
    sine = jnp.sin(angle)
    first_half = vectors[..., :half]
    second_half = vectors[..., half:]
    return jnp.concatenate(
        [first_half * cosine - second_half * sine, second_half * cosine + first_half * sine],
        axis=-1,
    )


def partial_softmax(queries, keys, values, valid):
    scores = (
        jnp.einsum("rskgd,rpkd->rskgp", queries, keys, preferred_element_type=jnp.float32)
        * score_factor
    )
    maxima = jnp.max(jnp.where(valid, scores, masked_floor), axis=-1)
    expo = jnp.exp(jnp.where(valid, scores - maxima[..., None], masked_floor))
    totals = jnp.sum(expo, axis=-1)
    outputs = jnp.einsum(
        "rskgp,rpkd->rskgd", expo.astype(jnp.bfloat16), values, preferred_element_type=jnp.float32
    )
    return (maxima, totals, outputs)


def shards(
    token_ids,
    cache_lengths,
    embed_table,
    key_cache,
    value_cache,
    norm_attn,
    norm_mlp,
    w_qkv,
    w_out,
    w_gate,
    w_up,
    w_down,
):
    place = lax.axis_index("seq")
    req_all = token_ids.shape[0]
    steps = token_ids.shape[1]
    ctx_own = key_cache.shape[1]
    att_width = H * HD
    kv_width = KVH * HD
    group = H // KVH
    picked = jnp.take(embed_table, token_ids.reshape(-1), axis=1)
    whole = lax.all_gather(picked, "seq", axis=0, tiled=True)
    resid = (
        jnp.transpose(whole, (1, 0)).reshape(req_all, steps, -1).astype(jnp.float32) * embed_factor
    )
    slot_pos = place * ctx_own + jnp.arange(ctx_own, dtype=jnp.int32)
    cache_valid = (slot_pos[None, :] < cache_lengths[:, None]).reshape(req_all, 1, 1, 1, ctx_own)
    cache_keys = key_cache.reshape(req_all, ctx_own, KVH, HD)
    cache_values = value_cache.reshape(req_all, ctx_own, KVH, HD)
    normed = rms_scale(resid, norm_attn).astype(jnp.bfloat16)
    qkv_cols = jnp.einsum("rsd,dc->rsc", normed, w_qkv, preferred_element_type=jnp.float32).astype(
        jnp.bfloat16
    )
    qkv_all = lax.all_gather(qkv_cols, "seq", axis=2, tiled=True)
    where = (cache_lengths[:, None] + jnp.arange(steps, dtype=jnp.int32)[None, :]).astype(
        jnp.float32
    )
    queries = rotate(
        qkv_all[..., :att_width].reshape(req_all, steps, H, HD).astype(jnp.float32),
        where[..., None],
    ).astype(jnp.bfloat16)
    keys_new = rotate(
        qkv_all[..., att_width : att_width + kv_width]
        .reshape(req_all, steps, KVH, HD)
        .astype(jnp.float32),
        where[..., None],
    ).astype(jnp.bfloat16)
    values_new = qkv_all[..., att_width + kv_width :].reshape(req_all, steps, KVH, HD)
    grouped = queries.reshape(req_all, steps, KVH, group, HD)
    cache_max, cache_total, cache_out = partial_softmax(
        grouped, cache_keys, cache_values, cache_valid
    )
    fresh_valid = (
        jnp.arange(steps, dtype=jnp.int32)[None, :] <= jnp.arange(steps, dtype=jnp.int32)[:, None]
    ).reshape(1, steps, 1, 1, steps)
    fresh_max, fresh_total, fresh_out = partial_softmax(grouped, keys_new, values_new, fresh_valid)
    overall = jnp.maximum(lax.pmax(cache_max, "seq"), fresh_max)
    cache_scale = jnp.exp(cache_max - overall)
    packed = jnp.concatenate(
        [cache_scale[..., None] * cache_out, (cache_scale * cache_total)[..., None]], axis=-1
    )
    summed = lax.psum(packed, "seq")
    fresh_scale = jnp.exp(fresh_max - overall)
    numer = summed[..., :HD] + fresh_scale[..., None] * fresh_out
    denom = summed[..., HD] + fresh_scale * fresh_total
    attention = (numer / denom[..., None]).astype(jnp.bfloat16).reshape(req_all, steps, att_width)
    proj_cols = jnp.einsum(
        "rsa,ac->rsc", attention, w_out, preferred_element_type=jnp.float32
    ).astype(jnp.bfloat16)
    projected = lax.all_gather(proj_cols, "seq", axis=2, tiled=True)
    middle = resid + branch_factor * projected.astype(jnp.float32)
    normed_mlp = rms_scale(middle, norm_mlp).astype(jnp.bfloat16)
    gate = jnp.einsum("rsd,df->rsf", normed_mlp, w_gate, preferred_element_type=jnp.float32)
    upward = jnp.einsum("rsd,df->rsf", normed_mlp, w_up, preferred_element_type=jnp.float32)
    hidden = (jax.nn.silu(gate) * upward).astype(jnp.bfloat16)
    down_part = jnp.einsum("rsf,fd->rsd", hidden, w_down, preferred_element_type=jnp.float32)
    down = lax.psum(down_part, "seq")
    return (middle + branch_factor * down).astype(jnp.bfloat16)


def solution(mesh):
    return jax.shard_map(
        shards,
        mesh=mesh,
        in_specs=(
            P("rep", None),
            P("rep"),
            P("seq", None),
            P("rep", "seq", None),
            P("rep", "seq", None),
            P(),
            P(),
            P(None, "seq"),
            P(None, "seq"),
            P(None, "seq"),
            P(None, "seq"),
            P("seq", None),
        ),
        out_specs=P("rep", None, None),
        check_vma=False,
    )
```

profile of v0, /device:TPU:1, one launch (start us, length us, event | category | flops | bytes accessed | tf_op | source)
XLA Modules:
  0.0 811.6 jit_solution(16249509916441426397)
XLA Ops:
  6.5 0.8 reshape.176
  7.4 0.8 reshape.175
  8.2 6.4 copy.89
  14.6 4.2 gather_fusion
  18.9 51.6 %all-gather = bf16[64,32,16]{1,2,0:T(8,128)(2,1)S(1)} all-gather(bf16[1,32,16]{1,2,0:T(8,128)(2,1)S(1)} %select_bitcast_fusion), channel_id=1, replica_groups=mesh['seq'=64,'rep'=8] {'seq'}, dimensions={0}, use_global_device_ids=true | all-gather | bytes 66560 | tf_op jit(solution)/shard_map/all_gather | solution.py:73
  70.4 0.3 copy.90
  71.9 51.1 %all_gather.10 = bf16[4,4,3072]{1,0,2:T(4,128)(2,1)S(1)} all-gather(bf16[4,4,48]{1,0,2:T(4,128)(2,1)S(1)} %copy.92), channel_id=1, replica_groups=mesh['seq'=64,'rep'=8] {'seq'}, dimensions={2}, use_global_device_ids=true | all-gather | bytes 99840 | tf_op jit(solution)/shard_map/all_gather | solution.py:85
  123.0 0.7 slice.38
  123.8 1.2 fusion.44
  124.9 2.2 copy.124
  127.1 1.0 reshape.182
  128.2 0.3 copy.125
  128.8 1.3 copy.96
  130.6 0.4 select_reduce_fusion.1
  131.0 243.2 %pmax.7 = f32[4,4,8,4]{3,1,2,0:T(4,128)S(1)} all-reduce(f32[4,4,8,4]{3,1,2,0:T(4,128)S(1)} %get-tuple-element.19), channel_id=1, replica_groups=mesh['seq'=64,'rep'=8] {'seq'}, use_global_device_ids=true, to_apply=%region_2.3 | all-reduce | flops 512 | bytes 4096 | tf_op jit(solution)/shard_map/pmax | solution.py:108
  374.2 0.4 fusion.16
  374.7 0.3 copy.100
  375.0 1.3 select_reduce_fusion
  376.4 0.9 copy.102
  377.3 0.5 fusion.1
  377.7 0.9 pad_maximum_fusion
  378.9 0.4 fusion.18
  379.3 185.2 %all-reduce.3.cloned.1.call-done = f32[4,4,8,4,65]{4,3,1,2,0:T(4,128)} async-done(((f32[4,4,8,4,65]{4,3,1,2,0:T(4,128)}), f32[4,4,8,4,65]{4,3,1,2,0:T(4,128)}) %all-reduce.3.cloned.1.call-update) | async-done | bytes 133136 | tf_op jit(solution)/shard_map/psum | solution.py:113
  564.5 1.1 slice.46
  565.7 0.9 copy.123
  566.6 1.6 fusion.6
  568.7 48.3 %all_gather.11 = bf16[4,4,2048]{1,0,2:T(4,128)(2,1)S(1)} all-gather(bf16[4,4,32]{1,0,2:T(4,128)(2,1)S(1)} %copy.109), channel_id=1, replica_groups=mesh['seq'=64,'rep'=8] {'seq'}, dimensions={2}, use_global_device_ids=true | all-gather | bytes 66560 | tf_op jit(solution)/shard_map/all_gather | solution.py:121
  617.0 1.3 copy.110
  618.5 1.3 fusion.12
  619.8 1.1 fusion.8
  620.9 182.2 %all-reduce.5.cloned.1.call-done = f32[4,4,2048]{2,1,0:T(4,128)} async-done(((f32[4,4,2048]{2,1,0:T(4,128)}), f32[4,4,2048]{2,1,0:T(4,128)}) %all-reduce.5.cloned.1.call-update) | async-done | bytes 131088 | tf_op jit(solution)/shard_map/psum | solution.py:128
  803.2 1.6 add_convert_fusion.1
  (55 shorter events, 3.1 us)
Async XLA Ops:
  6.5 613.2 %copy-start = (bf16[128,2048]{1,0:T(8,128)(2,1)S(1)}, bf16[128,2048]{1,0:T(8,128)(2,1)}, u32[]{:S(2)}) copy-start(bf16[128,2048]{1,0:T(8,128)(2,1)} %param.23) | copy-start | bytes 1572868
  6.5 558.0 %all-reduce.3.cloned.1.call-start = ((), (), s32[]{:S(2)}) async-start(), calls=%async_computation | async-start | bytes 524288 | tf_op jit(solution)/shard_map/psum | solution.py:113
  8.1 63.3 %copy-start.4 = (bf16[2048]{0:T(1024)(128)(2,1)S(1)}, bf16[2048]{0:T(1024)(128)(2,1)}, u32[]{:S(2)}) copy-start(bf16[2048]{0:T(1024)(128)(2,1)} %param.17) | copy-start | bytes 12292
  8.1 63.3 %copy-start.7 = (bf16[2048,48]{0,1:T(8,128)(2,1)S(1)}, bf16[2048,48]{0,1:T(8,128)(2,1)}, u32[]{:S(2)}) copy-start(bf16[2048,48]{0,1:T(8,128)(2,1)} %param.19) | copy-start | bytes 589828
  123.8 4.4 copy-start.6
  127.1 247.6 %copy-start.1 = (bf16[4,128,512]{2,1,0:T(8,128)(2,1)S(1)}, bf16[4,128,512]{2,1,0:T(8,128)(2,1)}, u32[]{:S(2)}) copy-start(bf16[4,128,512]{2,1,0:T(8,128)(2,1)} %param.16) | copy-start | bytes 1572868
  376.3 3.0 copy-start.5
  377.3 189.3 %copy-start.3 = (bf16[4,4,512]{1,0,2:T(4,128)(2,1)S(1)}, bf16[4,4,512]{1,0,2:T(4,128)(2,1)}, u32[]{:S(2)}) copy-start(bf16[4,4,512]{1,0,2:T(4,128)(2,1)} %get-tuple-element.10) | copy-start | bytes 49156
  378.7 424.5 %all-reduce.5.cloned.1.call-start = ((), (), s32[]{:S(2)}) async-start(), calls=%async_computation.1 | async-start | bytes 262144 | tf_op jit(solution)/shard_map/psum | solution.py:128
  379.3 189.1 %copy-start.8 = (bf16[2048,32]{0,1:T(8,128)(2,1)S(1)}, bf16[2048,32]{0,1:T(8,128)(2,1)}, u32[]{:S(2)}) copy-start(bf16[2048,32]{0,1:T(8,128)(2,1)} %param.20) | copy-start | bytes 393220
  568.2 51.6 %copy-start.2 = (bf16[2048,128]{1,0:T(8,128)(2,1)S(1)}, bf16[2048,128]{1,0:T(8,128)(2,1)}, u32[]{:S(2)}) copy-start(bf16[2048,128]{1,0:T(8,128)(2,1)} %param.22) | copy-start | bytes 1572868
Sparse Core Ops, SparseCore 0:
  378.8 185.6 all-reduce.2
  621.0 182.0 all-reduce.4
where the time goes:
time: 812 us
  blocking collectives  394 us (49%)
  waiting for transfers between devices  368 us (45%)
  local copies, waits for them, and re-layouts  24.9 us (3%)
  between operations  13.7 us (2%)
    pmax x1, blocking collectives, shards(): overall = jnp.maximum(lax.pmax(cache_max, 'seq'), fresh_max)  243 us
    psum x1, waiting for transfers between devices, shards(): summed = lax.psum(packed, 'seq')  185 us
    psum x1, waiting for transfers between devices, shards(): down = lax.psum(down_part, 'seq')  182 us
    all_gather x1, blocking collectives, shards(): whole = lax.all_gather(picked, 'seq', axis=0, tiled=True)  51.6 us
    all_gather x1, blocking collectives, shards(): qkv_all = lax.all_gather(qkv_cols, 'seq', axis=2, tiled=True)  51.1 us
    all_gather x1, blocking collectives, shards(): projected = lax.all_gather(proj_cols, 'seq', axis=2, tiled=True)  48.3 us
  transfers between devices with their start and end apart: 2, of which 2 were waited for; matrix products, arithmetic and copies ran while one was open for 0% of the time, Pallas kernels for 0%

commit v1 on v0

--- a/solution.py
+++ b/solution.py
@@ -13,6 +13,11 @@
 branch_factor = 0.22
 rope_base = 10000000.0
 masked_floor = -1e30
+
+
+def assign_packet(view, row_axis):
+    p_next = lax.all_gather(view, axis_name=row_axis)
+    return jnp.sum(p_next, 0)
 
 
 def rms_scale(resid, gain):
@@ -125,7 +130,7 @@
     upward = jnp.einsum("rsd,df->rsf", normed_mlp, w_up, preferred_element_type=jnp.float32)
     hidden = (jax.nn.silu(gate) * upward).astype(jnp.bfloat16)
     down_part = jnp.einsum("rsf,fd->rsd", hidden, w_down, preferred_element_type=jnp.float32)
-    down = lax.psum(down_part, "seq")
+    down = assign_packet(down_part, "seq")
     return (middle + branch_factor * down).astype(jnp.bfloat16)
 
 

time: 812 us -> 724 us (0.89)
  waiting for transfers between devices: 368 us -> 273 us
    psum x1 -> x0, waiting for transfers between devices: 182 us -> none  [shards(): down = lax.psum(down_part, 'seq')]
    all_gather x0 -> x1, waiting for transfers between devices: none -> 87.5 us  [assign_packet(): p_next = lax.all_gather(view, axis_name=row_axis)]
where the time goes in v1:
time: 724 us
  blocking collectives  394 us (54%)
  waiting for transfers between devices  273 us (38%)
  local copies, waits for them, and re-layouts  25.7 us (4%)
  between operations  13.7 us (2%)
  other arithmetic  9.65 us (1%)
  matrix products  7.54 us (1%)
    pmax x1, blocking collectives, shards(): overall = jnp.maximum(lax.pmax(cache_max, 'seq'), fresh_max)  243 us
    psum x1, waiting for transfers between devices, shards(): summed = lax.psum(packed, 'seq')  185 us
    all_gather x1, waiting for transfers between devices, assign_packet(): p_next = lax.all_gather(view, axis_name=row_axis)  87.5 us
    all_gather x1, blocking collectives, shards(): whole = lax.all_gather(picked, 'seq', axis=0, tiled=True)  51.6 us
    all_gather x1, blocking collectives, shards(): qkv_all = lax.all_gather(qkv_cols, 'seq', axis=2, tiled=True)  51.1 us
    all_gather x1, blocking collectives, shards(): projected = lax.all_gather(proj_cols, 'seq', axis=2, tiled=True)  48.3 us
  transfers between devices with their start and end apart: 2, of which 2 were waited for; matrix products, arithmetic and copies ran while one was open for 0% of the time, Pallas kernels for 0%

profile of v1, /device:TPU:1, one launch (start us, length us, event | category | flops | bytes accessed | tf_op | source)
XLA Modules:
  0.0 723.8 jit_solution(8158428959284720622)
XLA Ops:
  6.5 0.8 reshape.176
  7.4 0.8 reshape.175
  8.2 0.7 convert_element_type.75
  8.9 6.4 copy.116
  15.3 4.2 gather_fusion
  19.5 51.6 %all-gather.1 = bf16[64,32,16]{1,2,0:T(8,128)(2,1)S(1)} all-gather(bf16[1,32,16]{1,2,0:T(8,128)(2,1)S(1)} %select_bitcast_fusion), channel_id=1, replica_groups=mesh['seq'=64,'rep'=8] {'seq'}, dimensions={0}, use_global_device_ids=true | all-gather | bytes 66560 | tf_op jit(solution)/shard_map/all_gather | solution.py:78
  72.6 51.1 %all_gather.16 = bf16[4,4,3072]{1,0,2:T(4,128)(2,1)S(1)} all-gather(bf16[4,4,48]{1,0,2:T(4,128)(2,1)S(1)} %copy.119), channel_id=1, replica_groups=mesh['seq'=64,'rep'=8] {'seq'}, dimensions={2}, use_global_device_ids=true | all-gather | bytes 99840 | tf_op jit(solution)/shard_map/all_gather | solution.py:90
  123.7 1.2 fusion.44
  124.8 0.7 slice.38
  125.8 2.1 copy.123
  127.8 2.1 copy.127
  129.9 1.3 copy.151
  131.2 0.3 copy.152
  132.3 1.4 select_reduce_fusion.1
  133.7 243.2 %pmax.7 = f32[4,4,8,4]{3,1,2,0:T(4,128)S(1)} all-reduce(f32[4,4,8,4]{3,1,2,0:T(4,128)S(1)} %get-tuple-element.19), channel_id=1, replica_groups=mesh['seq'=64,'rep'=8] {'seq'}, use_global_device_ids=true, to_apply=%region_2.3 | all-reduce | flops 512 | bytes 4096 | tf_op jit(solution)/shard_map/pmax | solution.py:113
  377.0 0.4 fusion.16
  377.5 1.3 select_reduce_fusion
  378.8 0.9 copy.129
  379.7 0.5 fusion.1
  380.2 0.9 pad_maximum_fusion
  381.4 0.4 fusion.18
  381.8 185.2 %all-reduce.2.cloned.1.call-done = f32[4,4,8,4,65]{4,3,1,2,0:T(4,128)} async-done(((f32[4,4,8,4,65]{4,3,1,2,0:T(4,128)}), f32[4,4,8,4,65]{4,3,1,2,0:T(4,128)}) %all-reduce.2.cloned.1.call-update) | async-done | bytes 133136 | tf_op jit(solution)/shard_map/psum | solution.py:118
  567.0 1.1 slice.46
  568.1 0.9 copy.150
  569.1 1.6 fusion.6
  571.2 48.3 %all_gather.17 = bf16[4,4,2048]{1,0,2:T(4,128)(2,1)S(1)} all-gather(bf16[4,4,32]{1,0,2:T(4,128)(2,1)S(1)} %copy.136), channel_id=1, replica_groups=mesh['seq'=64,'rep'=8] {'seq'}, dimensions={2}, use_global_device_ids=true | all-gather | bytes 66560 | tf_op jit(solution)/shard_map/all_gather | solution.py:126
  619.5 1.3 copy.137
  620.9 1.3 fusion.12
  622.2 1.1 fusion.8
  623.4 87.5 %all-gather.4.cloned.1.call-done = f32[256,4,2048]{2,1,0:T(4,128)} async-done(((f32[4,4,2048]{2,1,0:T(4,128)}), f32[256,4,2048]{2,1,0:T(4,128)}) %all-gather.4.cloned.1.call-update) | async-done | bytes 8388624 | tf_op jit(solution)/shard_map/all_gather | solution.py:19
  710.9 5.3 reduce_sum.49
  716.2 0.7 add_convert_fusion.1
  (54 shorter events, 3.5 us)
Async XLA Ops:
  6.5 615.7 %copy-start = (bf16[128,2048]{1,0:T(8,128)(2,1)S(1)}, bf16[128,2048]{1,0:T(8,128)(2,1)}, u32[]{:S(2)}) copy-start(bf16[128,2048]{1,0:T(8,128)(2,1)} %param.23) | copy-start | bytes 1572868
  6.5 560.4 %all-reduce.2.cloned.1.call-start = ((), (), s32[]{:S(2)}) async-start(), calls=%async_computation | async-start | bytes 524288 | tf_op jit(solution)/shard_map/psum | solution.py:118
  8.9 63.3 %copy-start.6 = (bf16[2048,48]{0,1:T(8,128)(2,1)S(1)}, bf16[2048,48]{0,1:T(8,128)(2,1)}, u32[]{:S(2)}) copy-start(bf16[2048,48]{0,1:T(8,128)(2,1)} %param.19) | copy-start | bytes 589828
  123.7 1.9 copy-start.5
  131.2 248.6 %copy-start.2 = (bf16[4,128,512]{1,2,0:T(8,128)(2,1)S(1)}, bf16[4,128,512]{1,2,0:T(8,128)(2,1)}, u32[]{:S(2)}) copy-start(bf16[4,128,512]{1,2,0:T(8,128)(2,1)} %copy.127) | copy-start | bytes 1572868
  378.8 3.0 copy-start.4
  379.7 189.3 %copy-start.3 = (bf16[4,4,512]{1,0,2:T(4,128)(2,1)S(1)}, bf16[4,4,512]{1,0,2:T(4,128)(2,1)}, u32[]{:S(2)}) copy-start(bf16[4,4,512]{1,0,2:T(4,128)(2,1)} %get-tuple-element.10) | copy-start | bytes 49156
  381.1 329.7 %all-gather.4.cloned.1.call-start = ((), (), s32[]{:S(2)}) async-start(), calls=%async_computation.1 | async-start | bytes 8519680 | tf_op jit(solution)/shard_map/all_gather | solution.py:19
  381.7 189.1 %copy-start.7 = (bf16[2048,32]{0,1:T(8,128)(2,1)S(1)}, bf16[2048,32]{0,1:T(8,128)(2,1)}, u32[]{:S(2)}) copy-start(bf16[2048,32]{0,1:T(8,128)(2,1)} %param.20) | copy-start | bytes 393220
  570.7 51.6 %copy-start.1 = (bf16[2048,128]{1,0:T(8,128)(2,1)S(1)}, bf16[2048,128]{1,0:T(8,128)(2,1)}, u32[]{:S(2)}) copy-start(bf16[2048,128]{1,0:T(8,128)(2,1)} %param.22) | copy-start | bytes 1572868
Sparse Core Ops, SparseCore 0:
  381.3 185.6 all-reduce.1
  623.5 87.3 all-gather.3
